TPU v7x, 256 devices: a whole 4x4x8 slice. The times are simulated.
256 devices in a mesh: row: 32 (over z, y_lo, core), col: 8 (over y_hi, x).
Axes of the slice: x: 4, y: 4 (y_hi: 2, y_lo: 2; y = y_hi * 2 + y_lo), z: 8, core: 2. Of those that a mesh axis runs over, the one named last changes fastest.
Arguments:
- features: bfloat16 [32768, 128], P(('col', 'row')), may hold values from -96 to 96
- weight: bfloat16 [128, 256], replicated, may hold values from -0.5 to 0.5
- bias: float32 [256], replicated, may hold values from -3 to 3
- cotangent: bfloat16 [32768, 256], P(('row', 'col')), may hold values from -6 to 6
- tile_values: bfloat16 [32, 8, 256, 128, 128], P('row', 'col'), may hold values from 0 to 4, as said below
- tile_pos: int32 [32, 8, 2, 256], P('row', 'col'), may hold values from 0 to 31, as said below
- tile_count: int32 [32, 8], P('row', 'col'), may hold values from 0 to 256, as said below
- block_perm: int32 [256], replicated, may hold values from 0 to 255, as said below
Outputs:
- hidden: bfloat16 [32768, 256], P(('row', 'col'))
- weight_grad: float32 [128, 256], replicated
- bias_grad: float32 [256], replicated
Inputs may be any that keep to these rules, and one draw needn't show every extreme that they name: `tile_values`: entries are 0 or a weight of at least 0.25; slots t at or beyond tile_count[r, c] belong to no tile. `tile_pos`: entry [r, c, 0, t] is the slot's tile row, below 8, within row block r, and [r, c, 1, t] its tile column, below 32, within column block c, both in the reordered numbering; the slots of one cell hold distinct positions. `tile_count`: every draw has a cell with 256 live slots. `block_perm`: each aligned run of 8 entries is a permutation of that run's own indices.
All inputs are finite; a program needn't handle non-finite values.
Results may differ from a plain program's by a relative error of at most 0.0059.
Values may be sent and summed in bfloat16 or wider, within the bound.
No kernel may reach another device: no remote copies, remote signals or barrier semaphores. Data moves between devices by JAX's collectives and lax.ppermute only.
A program may use at most 64 MiB of HBM per device.

v0:
```python
import jax
import jax.numpy as jnp
from jax import lax
from jax.sharding import PartitionSpec as P


def local_index(block_perm, tile_axis, block_index, run_length):
    return jnp.take(block_perm, block_index * run_length + tile_axis) - block_index * run_length


def body(features, weight, bias, cotangent, tile_values, tile_pos, tile_count, block_perm):
    row_count = lax.axis_size("row")
    col_count = lax.axis_size("col")
    row_index = lax.axis_index("row")
    col_index = lax.axis_index("col")
    packed = tile_values[0, 0]
    positions = tile_pos[0, 0]
    live_count = tile_count[0, 0]
    max_tiles = packed.shape[0]
    tile_size = packed.shape[1]
    feat_width = features.shape[1]
    row_tiles = block_perm.shape[0] // row_count
    col_tiles = row_tiles * row_count // col_count
    block_tiles = min(64, max_tiles)
    lane_index = jnp.arange(block_tiles, dtype=jnp.int32)
    own_rows = local_index(block_perm, positions[0], row_index, row_tiles)
    own_cols = local_index(block_perm, positions[1], col_index, col_tiles)

    def degree_step(block_step, totals):
        row_acc, col_acc = totals
        slot_number = block_step * block_tiles + lane_index
        is_live = slot_number < live_count
        clamped = jnp.minimum(slot_number, max_tiles - 1)
        values = jnp.take(packed, clamped, axis=0).astype(jnp.float32)
        row_part = jnp.sum(values, axis=2)
        col_part = jnp.sum(values, axis=1)
        row_part = jnp.where(is_live[:, None], row_part, 0.0)
        col_part = jnp.where(is_live[:, None], col_part, 0.0)
        row_acc = row_acc.at[jnp.take(own_rows, clamped)].add(row_part)
        col_acc = col_acc.at[jnp.take(own_cols, clamped)].add(col_part)
        return (row_acc, col_acc)

    degree_blocks = (live_count + block_tiles - 1) // block_tiles
    row_acc, col_acc = lax.fori_loop(
        jnp.int32(0),
        degree_blocks,
        degree_step,
        (
            jnp.zeros((row_tiles, tile_size), jnp.float32),
            jnp.zeros((col_tiles, tile_size), jnp.float32),
        ),
    )
    col_part_flat = col_acc.reshape(col_tiles * tile_size)
    col_share = lax.psum_scatter(col_part_flat, "row", scatter_dimension=0, tiled=True)
    scaled = (lax.rsqrt(1.0 + col_share)[:, None] * features.astype(jnp.float32)).astype(
        jnp.bfloat16
    )
    gathered = lax.all_gather(scaled, "row", axis=0, tiled=True)
    feature_tiles = gathered.reshape(col_tiles, tile_size, feat_width)
    list_length = packed.shape[0]

    def product_step(block_step, partial_value):
        logical = block_step * block_tiles + lane_index
        is_live = logical < live_count
        is_upper = logical >= live_count
        source = jnp.where(is_upper, logical - live_count, logical)
        source = jnp.clip(source, 0, list_length - 1)
        slot_number = jnp.minimum(is_upper.astype(jnp.int32), 1 - 1)
        tile_block = jnp.take(packed, source, axis=0)
        tile_block = jnp.where(is_live[:, None, None], tile_block, jnp.zeros((), jnp.bfloat16))
        inputs = jnp.take(feature_tiles, jnp.take(own_cols, source), axis=0)
        products = jnp.einsum(
            "bpq,bqf->bpf", tile_block, inputs, preferred_element_type=jnp.float32
        )
        return partial_value.at[slot_number, jnp.take(own_rows, source)].add(products)

    product_blocks = (live_count + block_tiles - 1) // block_tiles
    initial = jnp.zeros((1, row_tiles, tile_size, feat_width), jnp.float32)
    partial_value = lax.fori_loop(jnp.int32(0), product_blocks, product_step, initial)
    own_sum = partial_value[0]
    row_part_flat = row_acc.reshape(row_tiles * tile_size)
    summed, degree_share = (
        lax.psum_scatter(
            own_sum.reshape(row_tiles * tile_size, feat_width),
            "col",
            scatter_dimension=0,
            tiled=True,
        ),
        lax.psum_scatter(row_part_flat, "col", scatter_dimension=0, tiled=True),
    )
    aggregated = (lax.rsqrt(1.0 + degree_share)[:, None] * summed).astype(jnp.bfloat16)
    preact = jnp.dot(aggregated, weight, preferred_element_type=jnp.float32) + bias
    logistic = jax.nn.sigmoid(preact)
    hidden = (preact * logistic).astype(jnp.bfloat16)
    preact_grad = (
        cotangent.astype(jnp.float32) * logistic * (1.0 + preact * (1.0 - logistic))
    ).astype(jnp.bfloat16)
    weight_part = jnp.einsum(
        "nf,nh->fh", aggregated, preact_grad, preferred_element_type=jnp.float32
    )
    bias_part = jnp.sum(preact_grad.astype(jnp.float32), axis=0)
    weight_sum, bias_sum = lax.psum((weight_part, bias_part), ("row", "col"))
    inverse_root = lax.rsqrt(jnp.float32(summed.shape[0] * row_count * col_count))
    return (hidden, weight_sum * inverse_root, bias_sum * inverse_root)


def solution(mesh):
    placed = (
        P(("col", "row"), None),
        P(),
        P(),
        P(("row", "col"), None),
        P("row", "col", None, None, None),
        P("row", "col", None, None),
        P("row", "col"),
        P(),
    )
    return jax.shard_map(
        body,
        mesh=mesh,
        in_specs=placed,
        out_specs=(P(("row", "col"), None), P(), P()),
        check_vma=False,
    )
```

profile of v0, /device:TPU:2, one launch (start us, length us, event | category | flops | bytes accessed | tf_op | source)
XLA Modules:
  0.0 723.7 jit_solution(14614431443404107920)
XLA Ops:
  8.7 2.0 gather_fusion.8
  10.7 2.0 gather_fusion.7
  12.7 9.5 %while.24 = (s32[]{:T(128)}, f32[8,128]{1,0:T(8,128)S(1)}, f32[32,128]{1,0:T(8,128)S(1)}, s32[]{:T(128)}, s32[256]{0:T(256)S(1)}, /*index=5*/s32[]{:T(128)}, bf1...) while((s32[]{:T(128)}, f32[8,128]{1,0:T(8,128)S(1)}, ...), condition=%wide.region_5.9_spmd.clone, body=%wide.region_0.8_spmd.clone.sunk | while | flops 4213635 | bytes 6451793 | solution.py:44
  13.4 0.8 gather_fusion.1
  14.2 0.8 gather_fusion
  15.0 4.3 gather_fusion.2
  19.4 0.9 convert_reduce_fusion.4
  20.2 1.0 scatter_custom_fusion.15
  21.2 1.0 scatter_custom_fusion.16
  22.2 122.7 %all-reduce.1 = f32[4096]{0:T(1024)S(1)} all-reduce(f32[4096]{0:T(1024)S(1)} %bitcast.44), channel_id=3, replica_groups=mesh['row'=32,'col'=8] {'row'}, use_global_device_ids=true, to_apply=%region_7.11.clone | all-reduce | flops 4096 | bytes 32768
  147.1 74.5 %all-gather.2.cloned.1.call-done = bf16[4096,128]{1,0:T(8,128)(2,1)} async-done(((bf16[128,128]{1,0:T(8,128)(2,1)}), bf16[4096,128]{1,0:T(8,128)(2,1)}) %all-gather.2.cloned.1.call-update) | async-done | bytes 1048592 | tf_op jit(solution)/shard_map/all_gather | solution.py:58
  221.6 24.0 %while.25 = (s32[]{:T(128)}, f32[1,8,128,128]{3,2,1,0:T(8,128)S(1)}, s32[]{:T(128)}, s32[]{:T(128)}, s32[256]{0:T(256)S(1)}, /*index=5*/bf16[256,128,128]{2,1,0:...) while((s32[]{:T(128)}, f32[1,8,128,128]{3,2,1,0:T(8,128)S(1)}, ...), condition=%wide.region_10.14_spmd.clone, body=%wide.region_8.13_spmd.clone.sunk | while | flops 272634240 | bytes 41956408 | solution.py:79
  223.2 0.8 gather_fusion.3
  224.7 2.2 gather_fusion.6
  226.8 5.7 gather_fusion.4
  232.5 4.3 fusion.45
  236.8 8.8 %scatter_fusion = f32[8,128,128]{2,1,0:T(8,128)S(1)} fusion(f32[8,128,128]{2,1,0:T(8,128)S(1)} %bitcast.39, s32[64]{0:T(128)S(1)} %fusion.44, f32[64,128,128]{2,1,0:T(8,128)} %fusion.45), kind=kCustom, calls=%fused_computation.11.clone.clone.1 | custom fusion | flops 1048576 | bytes 12583168 | tf_op jit(solution)/shard_map/while/body/scatter-add | solution.py:75
  247.7 43.6 %all-reduce = f32[1024]{0:T(1024)S(1)} all-reduce(f32[1024]{0:T(1024)S(1)} %bitcast.45), channel_id=2, replica_groups=mesh['row'=32,'col'=8] {'col'}, use_global_device_ids=true, to_apply=%region_6.10.clone | all-reduce | flops 1024 | bytes 8192
  291.4 102.7 %reduce-scatter.2.cloned.1.call-done = f32[128,128]{1,0:T(8,128)} async-done(((f32[1024,128]{1,0:T(8,128)}), f32[128,128]{1,0:T(8,128)}) %reduce-scatter.2.cloned.1.call-update) | async-done | bytes 65552 | tf_op jit(solution)/shard_map/reduce_scatter | solution.py:83
  394.1 1.7 convert_reduce_fusion.2
  395.8 73.9 %psum.15 = f32[256]{0:T(256)S(1)} all-reduce(f32[256]{0:T(256)S(1)} %get-tuple-element.182), channel_id=1, replica_groups=mesh['row'=32,'col'=8] {'row','col'}, use_global_device_ids=true, to_apply=%region_14.18 | all-reduce | flops 256 | bytes 2048 | tf_op jit(solution)/shard_map/psum | solution.py:102
  469.8 1.8 fusion.33
  472.1 243.5 %all-reduce.4.cloned.1.call-done = f32[128,256]{1,0:T(8,128)} async-done(((f32[128,256]{1,0:T(8,128)}), f32[128,256]{1,0:T(8,128)}) %all-reduce.4.cloned.1.call-update) | async-done | bytes 131088 | tf_op jit(solution)/shard_map/psum | solution.py:102
  715.6 1.6 broadcast_multiply_fusion
  (49 shorter events, 7.3 us)
Async XLA Ops:
  7.2 386.9 %copy-start = (bf16[128,256]{1,0:T(8,128)(2,1)S(1)}, bf16[128,256]{1,0:T(8,128)(2,1)}, u32[]{:S(2)}) copy-start(bf16[128,256]{1,0:T(8,128)(2,1)} %param.19) | copy-start | bytes 196612
  7.2 214.3 %all-gather.2.cloned.1.call-start = ((), (), s32[]{:S(2)}) async-start(), calls=%async_computation.1 | async-start | bytes 1081344 | tf_op jit(solution)/shard_map/all_gather | solution.py:58
  12.7 132.3 %copy-start.8 = (u32[256]{0:T(256)S(1)}, u32[256]{0:T(256)}, u32[]{:S(2)}) copy-start(u32[256]{0:T(256)} %constant.133) | copy-start | bytes 3076
  12.7 133.6 %copy-start.4 = (bf16[128,128]{1,0:T(8,128)(2,1)S(1)}, bf16[128,128]{1,0:T(8,128)(2,1)}, u32[]{:S(2)}) copy-start(bf16[128,128]{1,0:T(8,128)(2,1)} %param.18) | copy-start | bytes 98308
  12.7 381.4 %copy-start.5 = (bf16[128,256]{1,0:T(8,128)(2,1)S(1)}, bf16[128,256]{1,0:T(8,128)(2,1)}, u32[]{:S(2)}) copy-start(bf16[128,256]{1,0:T(8,128)(2,1)} %param.21) | copy-start | bytes 196612
  147.0 247.1 %reduce-scatter.2.cloned.1.call-start = ((), (), s32[]{:S(2)}) async-start(), calls=%async_computation.2 | async-start | bytes 589824 | tf_op jit(solution)/shard_map/reduce_scatter | solution.py:83
  221.6 24.9 %copy-start.7 = (u32[256]{0:T(256)S(1)}, u32[256]{0:T(256)}, u32[]{:S(2)}) copy-start(u32[256]{0:T(256)} %constant.129) | copy-start | bytes 3076
  221.6 172.5 %copy-start.6 = (f32[256]{0:T(256)S(1)}, f32[256]{0:T(256)}, u32[]{:S(2)}) copy-start(f32[256]{0:T(256)} %param.20) | copy-start | bytes 3076
  221.6 3.1 copy-start.2
  226.8 5.7 copy-start.3
  245.6 0.8 copy-start.1
  246.4 469.2 %all-reduce.4.cloned.1.call-start = ((), (), s32[]{:S(2)}) async-start(), calls=%async_computation.3 | async-start | bytes 262144 | tf_op jit(solution)/shard_map/psum | solution.py:102
Sparse Core Ops, SparseCore 0:
  147.1 74.3 all-gather.1
  246.6 147.4 reduce-scatter.1
  471.7 243.8 all-reduce.3
where the time goes:
time: 725 us; the launch traced here: 724 us
  waiting for transfers between devices  421 us (58%)
  blocking collectives  240 us (33%)
  local copies, waits for them, and re-layouts  21.3 us (3%)
  other arithmetic  17.5 us (2%)
  between operations  15.9 us (2%)
  matrix products  7.81 us (1%)
    psum x1, waiting for transfers between devices, body(): weight_sum, bias_sum = lax.psum((weight_part, bias_part), ('row', 'col'))  243 us
    unnamed x2, blocking collectives  166 us
    reduce_scatter x1, waiting for transfers between devices, body(): lax.psum_scatter(own_sum.reshape(row_tiles * tile_size, feat_width), 'col...  103 us
    all_gather x1, waiting for transfers between devices, body(): gathered = lax.all_gather(scaled, 'row', axis=0, tiled=True)  74.5 us
    psum x1, blocking collectives, body(): weight_sum, bias_sum = lax.psum((weight_part, bias_part), ('row', 'col'))  73.9 us
  transfers between devices with their start and end apart: 3, of which 3 were waited for; matrix products, arithmetic and copies ran while one was open for 0% of the time, Pallas kernels for 0%

commit v1 on v0

--- a/solution.py
+++ b/solution.py
@@ -55,7 +55,9 @@
     scaled = (lax.rsqrt(1.0 + col_share)[:, None] * features.astype(jnp.float32)).astype(
         jnp.bfloat16
     )
-    gathered = lax.all_gather(scaled, "row", axis=0, tiled=True)
+    gathered = jnp.concatenate(
+        lax.all_to_all(jnp.stack([scaled] * lax.axis_size("row")), "row", 0, 0), axis=0
+    )
     feature_tiles = gathered.reshape(col_tiles, tile_size, feat_width)
     list_length = packed.shape[0]
 

time: 725 us -> 695 us (0.959)
  waiting for transfers between devices: 421 us -> 345 us
  blocking collectives: 240 us -> 285 us
    all_gather x1 -> x0, waiting for transfers between devices: 74.5 us -> none  [body(): gathered = lax.all_gather(scaled, 'row', axis=0, tiled=True)]
    all_to_all x0 -> x1, blocking collectives: none -> 47.1 us  [body(): lax.all_to_all(jnp.stack([scaled] * lax.axis_size('row')), 'row', 0, 0)]
  transfers between devices with their start and end apart: 3 -> 2, of which waited for: 3 -> 2; matrix products, arithmetic and copies ran while one was open for 0% -> 0% of each run, Pallas kernels for 0% -> 0%
where the time goes in v1:
time: 695 us; the launch traced here: 693 us
  waiting for transfers between devices  345 us (50%)
  blocking collectives  285 us (41%)
  local copies, waits for them, and re-layouts  21.4 us (3%)
  other arithmetic  16.8 us (2%)
  between operations  16.2 us (2%)
  matrix products  8.42 us (1%)
    psum x1, waiting for transfers between devices, body(): weight_sum, bias_sum = lax.psum((weight_part, bias_part), ('row', 'col'))  244 us
    unnamed x2, blocking collectives  164 us
    reduce_scatter x1, waiting for transfers between devices, body(): lax.psum_scatter(own_sum.reshape(row_tiles * tile_size, feat_width), 'col...  102 us
    psum x1, blocking collectives, body(): weight_sum, bias_sum = lax.psum((weight_part, bias_part), ('row', 'col'))  73.9 us
    all_to_all x1, blocking collectives, body(): lax.all_to_all(jnp.stack([scaled] * lax.axis_size('row')), 'row', 0, 0)  47.1 us
  transfers between devices with their start and end apart: 2, of which 2 were waited for; matrix products, arithmetic and copies ran while one was open for 0% of the time, Pallas kernels for 0%

profile of v1, /device:TPU:2, one launch (start us, length us, event | category | flops | bytes accessed | tf_op | source)
XLA Modules:
  0.0 693.4 jit_solution(3747786525189773888)
XLA Ops:
  8.7 2.0 gather_fusion.8
  10.7 2.0 gather_fusion.7
  12.7 9.5 %while.24 = (s32[]{:T(128)}, f32[8,128]{1,0:T(8,128)S(1)}, f32[32,128]{1,0:T(8,128)S(1)}, s32[]{:T(128)}, s32[256]{0:T(256)S(1)}, /*index=5*/s32[]{:T(128)}, bf1...) while((s32[]{:T(128)}, f32[8,128]{1,0:T(8,128)S(1)}, ...), condition=%wide.region_5.9_spmd.clone, body=%wide.region_0.8_spmd.clone.sunk | while | flops 4213635 | bytes 6451793 | solution.py:44
  13.4 0.8 gather_fusion.1
  14.2 0.8 gather_fusion
  15.0 4.3 gather_fusion.2
  19.4 0.9 convert_reduce_fusion.4
  20.2 1.0 scatter_custom_fusion.15
  21.2 1.0 scatter_custom_fusion.16
  22.2 122.7 %all-reduce.1 = f32[4096]{0:T(1024)S(1)} all-reduce(f32[4096]{0:T(1024)S(1)} %bitcast.42), channel_id=3, replica_groups=mesh['row'=32,'col'=8] {'row'}, use_global_device_ids=true, to_apply=%region_7.11.clone | all-reduce | flops 4096 | bytes 32768
  146.6 47.1 %all_to_all.5 = bf16[32,128,128]{2,1,0:T(8,128)(2,1)S(1)} all-to-all(bf16[32,128,128]{2,1,0:T(8,128)(2,1)S(1)} %stack.2), channel_id=1, replica_groups=mesh['row'=32,'col'=8] {'row'}, dimensions={0} | all-to-all | bytes 2097152 | tf_op jit(solution)/shard_map/all_to_all | solution.py:59
  193.8 24.4 %while.25 = (s32[]{:T(128)}, f32[1,8,128,128]{3,2,1,0:T(8,128)S(1)}, s32[]{:T(128)}, s32[]{:T(128)}, s32[256]{0:T(256)S(1)}, /*index=5*/bf16[256,128,128]{2,1,0:...) while((s32[]{:T(128)}, ...), condition=%wide.region_10.14_spmd.clone, body=%wide.region_8.13_spmd.clone.sunk | while | flops 272634240 | bytes 29373440 | solution.py:81
  195.3 0.8 gather_fusion.3
  196.8 2.2 gather_fusion.6
  199.0 5.5 gather_fusion.4
  204.5 4.9 fusion.45
  209.4 8.8 %scatter_fusion = f32[8,128,128]{2,1,0:T(8,128)S(1)} fusion(f32[8,128,128]{2,1,0:T(8,128)S(1)} %bitcast.38, s32[64]{0:T(128)S(1)} %fusion.44, f32[64,128,128]{2,1,0:T(8,128)} %fusion.45), kind=kCustom, calls=%fused_computation.11.clone.clone.1 | custom fusion | flops 1048576 | bytes 12583168 | tf_op jit(solution)/shard_map/while/body/scatter-add | solution.py:77
  220.3 41.4 %all-reduce = f32[1024]{0:T(1024)S(1)} all-reduce(f32[1024]{0:T(1024)S(1)} %bitcast.43), channel_id=2, replica_groups=mesh['row'=32,'col'=8] {'col'}, use_global_device_ids=true, to_apply=%region_6.10.clone | all-reduce | flops 1024 | bytes 8192
  261.8 101.6 %reduce-scatter.2.cloned.1.call-done = f32[128,128]{1,0:T(8,128)} async-done(((f32[1024,128]{1,0:T(8,128)}), f32[128,128]{1,0:T(8,128)}) %reduce-scatter.2.cloned.1.call-update) | async-done | bytes 65552 | tf_op jit(solution)/shard_map/reduce_scatter | solution.py:85
  363.4 1.7 convert_reduce_fusion.2
  365.2 73.9 %psum.15 = f32[256]{0:T(256)S(1)} all-reduce(f32[256]{0:T(256)S(1)} %get-tuple-element.182), channel_id=1, replica_groups=mesh['row'=32,'col'=8] {'row','col'}, use_global_device_ids=true, to_apply=%region_14.18 | all-reduce | flops 256 | bytes 2048 | tf_op jit(solution)/shard_map/psum | solution.py:104
  439.1 1.8 fusion.33
  441.4 243.6 %all-reduce.4.cloned.1.call-done = f32[128,256]{1,0:T(8,128)} async-done(((f32[128,256]{1,0:T(8,128)}), f32[128,256]{1,0:T(8,128)}) %all-reduce.4.cloned.1.call-update) | async-done | bytes 131088 | tf_op jit(solution)/shard_map/psum | solution.py:104
  685.0 1.6 broadcast_multiply_fusion
  (44 shorter events, 6.8 us)
Async XLA Ops:
  7.2 356.3 %copy-start = (bf16[128,256]{1,0:T(8,128)(2,1)S(1)}, bf16[128,256]{1,0:T(8,128)(2,1)}, u32[]{:S(2)}) copy-start(bf16[128,256]{1,0:T(8,128)(2,1)} %param.19) | copy-start | bytes 196612
  7.2 356.2 %reduce-scatter.2.cloned.1.call-start = ((), (), s32[]{:S(2)}) async-start(), calls=%async_computation.2 | async-start | bytes 589824 | tf_op jit(solution)/shard_map/reduce_scatter | solution.py:85
  12.7 132.2 %copy-start.6 = (u32[256]{0:T(256)S(1)}, u32[256]{0:T(256)}, u32[]{:S(2)}) copy-start(u32[256]{0:T(256)} %constant.133) | copy-start | bytes 3076
  12.7 133.6 %copy-start.2 = (bf16[128,128]{1,0:T(8,128)(2,1)S(1)}, bf16[128,128]{1,0:T(8,128)(2,1)}, u32[]{:S(2)}) copy-start(bf16[128,128]{1,0:T(8,128)(2,1)} %param.18) | copy-start | bytes 98308
  193.8 25.3 %copy-start.5 = (u32[256]{0:T(256)S(1)}, u32[256]{0:T(256)}, u32[]{:S(2)}) copy-start(u32[256]{0:T(256)} %constant.129) | copy-start | bytes 3076
  193.8 169.6 %copy-start.3 = (bf16[128,256]{1,0:T(8,128)(2,1)S(1)}, bf16[128,256]{1,0:T(8,128)(2,1)}, u32[]{:S(2)}) copy-start(bf16[128,256]{1,0:T(8,128)(2,1)} %param.21) | copy-start | bytes 196612
  193.8 169.6 %copy-start.4 = (f32[256]{0:T(256)S(1)}, f32[256]{0:T(256)}, u32[]{:S(2)}) copy-start(f32[256]{0:T(256)} %param.20) | copy-start | bytes 3076
  218.2 0.8 copy-start.1
  219.0 466.0 %all-reduce.4.cloned.1.call-start = ((), (), s32[]{:S(2)}) async-start(), calls=%async_computation.3 | async-start | bytes 262144 | tf_op jit(solution)/shard_map/psum | solution.py:104
Sparse Core Ops, SparseCore 0:
  219.1 144.2 reduce-scatter.1
  441.0 243.9 all-reduce.3
